TPU v7x, 512 devices: a whole 4x8x8 slice. The times are simulated.
512 devices in a mesh: ep: 16 (over z_hi, y), sp: 32 (over z_lo, x, core).
Axes of the slice: x: 4, y: 8, z: 8 (z_hi: 2, z_lo: 4; z = z_hi * 4 + z_lo), core: 2. Of those that a mesh axis runs over, the one named last changes fastest.
Arguments:
- grad_out: bfloat16 [65536, 4096], P(('ep', 'sp')), may hold values from -1.5 to 1.5
- routes: int32 [65536, 8], P(('ep', 'sp')), may hold values from 0 to 127, as said below
- gate: bfloat16 [65536, 8], P(('ep', 'sp')), may hold values from 0.049804688 to 1
- saved: bfloat16 [16, 32, 256, 3072], P('ep', 'sp'), may hold values from -6 to 6
- w_down: bfloat16 [16, 1536, 4096], P('ep', None, 'sp'), may hold values from -0.15625 to 0.15625
Outputs:
- grad_pre: bfloat16 [16, 32, 256, 3072], P('ep', 'sp')
- grad_gate: float32 [65536, 8], P(('ep', 'sp'))
Inputs may be any that keep to these rules, and one draw needn't show every extreme that they name: `routes`: each row names 8 different experts. In every block of 128 rows at most 16 rows name the same expert whose number is a multiple of 8, and in every block one such expert is named by exactly 16 rows; it is the same expert for all blocks whose indices agree modulo 32.
All inputs are finite; a program needn't handle non-finite values.
Results may differ from a plain program's by a relative error of at most 0.0029.
Values may be sent and summed in bfloat16 or wider, within the bound.
No kernel may reach another device: no remote copies, remote signals or barrier semaphores. Data moves between devices by JAX's collectives and lax.ppermute only.
A program may use at most 128 MiB of HBM per device.

v0:
```python
import math
import jax
import jax.numpy as jnp
from jax import lax
from jax.sharding import PartitionSpec as P

EXPERTS = 128


def side_by_side(arrays, axis, split_dim, concat_dim, along):
    widths = [math.prod(a.shape[along:]) for a in arrays]
    both = jnp.concatenate(
        [a.reshape(*a.shape[:along], w) for a, w in zip(arrays, widths)], axis=along
    )
    whole = lax.all_to_all(both, axis, split_axis=split_dim, concat_axis=concat_dim, tiled=True)
    tiles = jnp.split(whole, [sum(widths[:k]) for k in range(1, len(widths))], axis=along)
    return tuple((b.reshape(*whole.shape[:along], *a.shape[along:]) for a, b in zip(arrays, tiles)))


def on_device(grad_out, routes, gate, saved, w_down):
    ep_count = lax.axis_size("ep")
    experts_each = EXPERTS // ep_count
    model_width = grad_out.shape[1]
    slot_count = saved.shape[2]
    capacity = slot_count // ep_count
    hidden_units = saved.shape[3] // 2
    flight = routes % experts_each == 0
    owners = routes // experts_each
    wave_ids = jnp.arange(ep_count, dtype=jnp.int32)
    onehot = (owners[:, :, None] == wave_ids[None, None, :]) & flight[:, :, None]
    member = jnp.sum(onehot.astype(jnp.int32), axis=1)
    gate_by_expert = jnp.sum(
        onehot.astype(jnp.float32) * gate.astype(jnp.float32)[:, :, None], axis=1
    )
    places = jnp.cumsum(member, axis=0) - member
    place_ids = jnp.arange(capacity, dtype=jnp.int32)
    chosen = (places.T[:, None, :] == place_ids[None, :, None]) & (member.T[:, None, :] > 0)
    chosen_float = chosen.astype(jnp.float32)
    outgoing = jnp.einsum(
        "fct,td->fcd", chosen.astype(jnp.bfloat16), grad_out, preferred_element_type=jnp.float32
    ).astype(jnp.bfloat16)
    gate_out = jnp.einsum(
        "fct,tf->fc", chosen_float, gate_by_expert, precision=lax.Precision.HIGHEST
    ).astype(jnp.bfloat16)
    gate_pre = saved[0, 0, :, :hidden_units].astype(jnp.float32)
    up_pre = saved[0, 0, :, hidden_units:].astype(jnp.float32)
    sigmoid_gate = jax.nn.sigmoid(gate_pre)
    silu_gate = gate_pre * sigmoid_gate
    hidden = (silu_gate * up_pre).astype(jnp.bfloat16)
    arrived, gate_in = side_by_side((outgoing, gate_out), "ep", 0, 0, 2)
    arrived = arrived.reshape(slot_count, model_width)
    gate_in = gate_in.reshape(slot_count).astype(jnp.float32)
    grad_hidden = lax.dot_general(
        arrived,
        lax.all_gather(w_down, "sp", axis=2, tiled=True)[0],
        (((1,), (1,)), ((), ())),
        preferred_element_type=jnp.float32,
    )
    score_values = jnp.sum(
        grad_hidden * lax.optimization_barrier(hidden).astype(jnp.float32), axis=1
    )
    scaled = grad_hidden * gate_in[:, None]
    grad_gate_pre = scaled * up_pre * sigmoid_gate * (1.0 + gate_pre * (1.0 - sigmoid_gate))
    grad_up_pre = scaled * silu_gate
    grad_pre = (
        jnp.concatenate([grad_gate_pre, grad_up_pre], axis=1)
        .astype(jnp.bfloat16)
        .reshape(saved.shape)
    )
    returned = lax.all_to_all(
        score_values.reshape(ep_count, capacity), "ep", split_axis=0, concat_axis=0, tiled=True
    )
    score_by_expert = jnp.einsum(
        "fct,fc->tf", chosen_float, returned, precision=lax.Precision.HIGHEST
    )
    grad_gate = jnp.sum(onehot.astype(jnp.float32) * score_by_expert[:, None, :], axis=2)
    return (grad_pre, grad_gate)


def solution(mesh):
    in_specs = (
        P(("ep", "sp"), None),
        P(("ep", "sp"), None),
        P(("ep", "sp"), None),
        P("ep", "sp", None, None),
        P("ep", None, "sp"),
    )
    out_specs = (P("ep", "sp", None, None), P(("ep", "sp"), None))
    return jax.shard_map(
        on_device, mesh=mesh, in_specs=in_specs, out_specs=out_specs, check_vma=False
    )
```

profile of v0, /device:TPU:1, one launch (start us, length us, event | category | flops | bytes accessed | tf_op | source)
XLA Modules:
  0.0 214.4 jit_solution(14429993677092649671)
XLA Ops:
  7.2 0.7 all-gather.2.cloned.1.call-update
  7.9 0.7 fusion.27
  8.6 0.7 add_select_fusion.1
  9.3 0.1 copy.18
  9.4 0.2 reduce_window_sum.11
  9.7 0.7 convert_element_type.54
  10.4 0.2 fusion.16
  10.7 0.2 copy.21
  10.8 0.7 convolution_convert_fusion
  11.5 1.5 pad_maximum_fusion
  13.1 16.2 %all-to-all-start = ((bf16[16,16,4097]{2,1,0:T(8,128)(2,1)}), bf16[16,16,4097]{2,1,0:T(8,128)(2,1)S(1)}, u32[]{:S(2)}, u32[]{:S(2)}) async-start(bf16[16,16,4097]{2,1,0:T(8,128)(2,1)} %pad_maximum_fusion), calls=%async_computation | async-start | bytes 4325376 | tf_op jit(solution)/shard_map/all_to_all | solution.py:15
  29.3 2.9 %fusion.5 = bf16[256,1536]{1,0:T(8,128)(2,1)} fusion(bf16[1,1,256,3072]{3,2,1,0:T(8,128)(2,1)} %param.8), kind=kLoop, calls=%fused_computation.12 | loop fusion | flops 3145728 | bytes 2359296 | tf_op jit(solution)/shard_map/convert_element_type | solution.py:49
  32.2 54.8 %all-to-all-done = bf16[16,16,4097]{2,1,0:T(8,128)(2,1)S(1)} async-done(((bf16[16,16,4097]{2,1,0:T(8,128)(2,1)}), bf16[16,16,4097]{2,1,0:T(8,128)(2,1)S(1)}, u32[]{:S(2)}, u32[]{:S(2)}) %all-to-all-start) | async-done | bytes 2097696 | tf_op jit(solution)/shard_map/all_to_all | solution.py:15
  86.9 0.1 convert_reduce_fusion
  87.0 0.1 reshape.66
  87.1 1.6 split.8
  88.7 81.5 %all-gather.2.cloned.1.call-done = bf16[1,1536,4096]{2,1,0:T(8,128)(2,1)} async-done(((bf16[1,1536,128]{2,1,0:T(8,128)(2,1)}), bf16[1,1536,4096]{2,1,0:T(8,128)(2,1)}) %all-gather.2.cloned.1.call-update) | async-done | bytes 12582928 | tf_op jit(solution)/shard_map/all_gather | solution.py:55
  170.2 10.0 %fusion.12 = (bf16[1,1,256,1536]{3,2,1,0:T(8,128)(2,1)S(1)}, bf16[1,1,256,1536]{3,2,1,0:T(8,128)(2,1)S(1)}, f32[256]{0:T(256)S(1)}) fusion(f32[256]{0:T(256)S(1)} %reshape.66, bf16[1,1,256,3072]{3,2,1,0:T(8,128)(2,1)} %param.8, bf16[256,1536]{1,0:T(8,128)(2,1)} %fusion.5, bf16[256,4096]{1,0:T(8,128)(2,1)} %bitcast.52, ...), kind=kOutput, calls=%fused_computation.22 | convolution fusion | flops 3228696320 | bytes 18614272 | tf_op jit(solution)/shard_map/dot_general | solution.py:53
  180.2 0.7 all_to_all.12
  180.9 14.5 %all-to-all-start.1 = ((f32[16,1,16]{2,1,0:T(1,128)}), f32[16,1,16]{2,1,0:T(1,128)S(1)}, u32[]{:S(2)}, u32[]{:S(2)}) async-start(f32[16,1,16]{2,1,0:T(1,128)} %all_to_all.12), calls=%async_computation.1 | async-start | bytes 16384 | tf_op jit(solution)/shard_map/all_to_all | solution.py:70
  195.4 1.4 pad_maximum_fusion.1
  196.8 9.9 %all-to-all-done.1 = f32[16,1,16]{2,1,0:T(1,128)S(1)} async-done(((f32[16,1,16]{2,1,0:T(1,128)}), f32[16,1,16]{2,1,0:T(1,128)S(1)}, u32[]{:S(2)}, u32[]{:S(2)}) %all-to-all-start.1) | async-done | bytes 1056 | tf_op jit(solution)/shard_map/all_to_all | solution.py:70
  206.7 0.2 fusion.14
  206.9 0.6 select_reduce_fusion
  (9 shorter events, 0.2 us)
Async XLA Ops:
  7.2 3.7 %copy-start = (bf16[128,4096]{1,0:T(8,128)(2,1)S(1)}, bf16[128,4096]{1,0:T(8,128)(2,1)}, u32[]{:S(2)}) copy-start(bf16[128,4096]{1,0:T(8,128)(2,1)} %param.5) | copy-start | bytes 3145732
  7.2 163.1 %all-gather.2.cloned.1.call-start = ((), (), s32[]{:S(2)}) async-start(), calls=%async_computation.2 | async-start | bytes 12976128 | tf_op jit(solution)/shard_map/all_gather | solution.py:55
  13.1 73.9 %all-to-all-start = ((bf16[16,16,4097]{2,1,0:T(8,128)(2,1)}), bf16[16,16,4097]{2,1,0:T(8,128)(2,1)S(1)}, u32[]{:S(2)}, u32[]{:S(2)}) async-start(bf16[16,16,4097]{2,1,0:T(8,128)(2,1)} %pad_maximum_fusion), calls=%async_computation | async-start | bytes 4325376 | tf_op jit(solution)/shard_map/all_to_all | solution.py:15
  180.9 25.8 %all-to-all-start.1 = ((f32[16,1,16]{2,1,0:T(1,128)}), f32[16,1,16]{2,1,0:T(1,128)S(1)}, u32[]{:S(2)}, u32[]{:S(2)}) async-start(f32[16,1,16]{2,1,0:T(1,128)} %all_to_all.12), calls=%async_computation.1 | async-start | bytes 16384 | tf_op jit(solution)/shard_map/all_to_all | solution.py:70
Sparse Core Ops, SparseCore 0:
  10.0 160.1 all-gather.1
where the time goes:
time: 215 us; the launch traced here: 214 us
  waiting for transfers between devices  147 us (68%)
  starting transfers between devices  30.7 us (14%)
  between operations  14.1 us (7%)
  matrix products  11.1 us (5%)
  other arithmetic  8.82 us (4%)
  local copies, waits for them, and re-layouts  2.74 us (1%)
    all_gather x1, waiting for transfers between devices, on_device(): lax.all_gather(w_down, 'sp', axis=2, tiled=True)[0]  81.5 us
    all_to_all x1, waiting for transfers between devices, side_by_side(): lax.all_to_all(both, axis, split_axis=split_dim, concat_axis=concat_dim,...  54.8 us
    all_to_all x1, starting transfers between devices, side_by_side(): lax.all_to_all(both, axis, split_axis=split_dim, concat_axis=concat_dim,...  16.2 us
    all_to_all x1, starting transfers between devices, on_device(): lax.all_to_all(score_values.reshape(ep_count, capacity), 'ep', split_axis...  14.5 us
    dot_general x1, matrix products, on_device(): lax.dot_general(arrived, lax.all_gather(w_down, 'sp', axis=2, tiled=True)...  9.98 us
    all_to_all x1, waiting for transfers between devices, on_device(): lax.all_to_all(score_values.reshape(ep_count, capacity), 'ep', split_axis...  9.89 us
  transfers between devices with their start and end apart: 3, of which 3 were waited for; matrix products, arithmetic and copies ran while one was open for 5% of the time, Pallas kernels for 0%

commit v1 on v0

--- a/solution.py
+++ b/solution.py
@@ -52,7 +52,9 @@
     gate_in = gate_in.reshape(slot_count).astype(jnp.float32)
     grad_hidden = lax.dot_general(
         arrived,
-        lax.all_gather(w_down, "sp", axis=2, tiled=True)[0],
+        jnp.concatenate(
+            lax.all_to_all(jnp.stack([w_down] * lax.axis_size("sp")), "sp", 0, 0), axis=2
+        )[0],
         (((1,), (1,)), ((), ())),
         preferred_element_type=jnp.float32,
     )

time: 215 us -> 416 us (1.93)
  waiting for transfers between devices: 147 us -> 339 us
  starting transfers between devices: 30.7 us -> 44.8 us
  between operations: 14.1 us -> 0.72 us
  local copies, waits for them, and re-layouts: 2.74 us -> 11.6 us
    all_to_all x0 -> x1, waiting for transfers between devices: none -> 274 us  [on_device(): lax.all_to_all(jnp.stack([w_down] * lax.axis_size('sp')), 'sp', 0, 0)]
    all_gather x1 -> x0, waiting for transfers between devices: 81.5 us -> none  [on_device(): lax.all_gather(w_down, 'sp', axis=2, tiled=True)[0]]
    all_to_all x0 -> x1, starting transfers between devices: none -> 9.08 us  [on_device(): lax.all_to_all(jnp.stack([w_down] * lax.axis_size('sp')), 'sp', 0, 0)]
    another operation x0 -> x2, local copies, waits for them, and re-layouts: none -> 8.8 us  [the longest x1 6.88 us: on_device(): jnp.stack([w_down] * lax.axis_size('sp'))]
    all_to_all x1, starting transfers between devices: 14.5 us -> 19.5 us  [on_device(): lax.all_to_all(score_values.reshape(ep_count, capacity), 'ep', split_axis...]
  transfers between devices with their start and end apart: 3 -> 3, of which waited for: 3 -> 3; matrix products, arithmetic and copies ran while one was open for 5% -> 2% of each run, Pallas kernels for 0% -> 0%
where the time goes in v1:
time: 416 us
  waiting for transfers between devices  339 us (81%)
  starting transfers between devices  44.8 us (11%)
  local copies, waits for them, and re-layouts  11.6 us (3%)
  matrix products  11 us (3%)
  other arithmetic  8.75 us (2%)
    all_to_all x1, waiting for transfers between devices, on_device(): lax.all_to_all(jnp.stack([w_down] * lax.axis_size('sp')), 'sp', 0, 0)  274 us
    all_to_all x1, waiting for transfers between devices, side_by_side(): lax.all_to_all(both, axis, split_axis=split_dim, concat_axis=concat_dim,...  54.7 us
    all_to_all x1, starting transfers between devices, on_device(): lax.all_to_all(score_values.reshape(ep_count, capacity), 'ep', split_axis...  19.5 us
    all_to_all x1, starting transfers between devices, side_by_side(): lax.all_to_all(both, axis, split_axis=split_dim, concat_axis=concat_dim,...  16.2 us
    dot_general x1, matrix products, on_device(): lax.dot_general(arrived, jnp.concatenate(lax.all_to_all(jnp.stack([w_down...  9.93 us
    all_to_all x1, waiting for transfers between devices, on_device(): lax.all_to_all(score_values.reshape(ep_count, capacity), 'ep', split_axis...  9.89 us
    all_to_all x1, starting transfers between devices, on_device(): lax.all_to_all(jnp.stack([w_down] * lax.axis_size('sp')), 'sp', 0, 0)  9.08 us
  transfers between devices with their start and end apart: 3, of which 3 were waited for; matrix products, arithmetic and copies ran while one was open for 2% of the time, Pallas kernels for 0%

profile of v1, /device:TPU:1, one launch (start us, length us, event | category | flops | bytes accessed | tf_op | source)
XLA Modules:
  0.0 416.0 jit_solution(16685171669435149848)
XLA Ops:
  0.6 0.8 add_select_fusion.1
  1.4 0.7 fusion.25
  2.3 0.2 reduce_window_sum.11
  2.5 0.7 convert_element_type.54
  3.2 0.2 fusion.14
  3.5 0.2 copy.30
  3.7 0.7 convolution_convert_fusion
  4.4 1.5 pad_maximum_fusion
  5.9 16.2 %all-to-all-start = ((bf16[16,16,4097]{2,1,0:T(8,128)(2,1)}), bf16[16,16,4097]{2,1,0:T(8,128)(2,1)S(1)}, u32[]{:S(2)}, u32[]{:S(2)}) async-start(bf16[16,16,4097]{2,1,0:T(8,128)(2,1)} %pad_maximum_fusion), calls=%async_computation | async-start | bytes 4325376 | tf_op jit(solution)/shard_map/all_to_all | solution.py:15
  22.1 1.9 copy.31
  24.0 54.7 %all-to-all-done = bf16[16,16,4097]{2,1,0:T(8,128)(2,1)S(1)} async-done(((bf16[16,16,4097]{2,1,0:T(8,128)(2,1)}), bf16[16,16,4097]{2,1,0:T(8,128)(2,1)S(1)}, u32[]{:S(2)}, u32[]{:S(2)}) %all-to-all-start) | async-done | bytes 2097696 | tf_op jit(solution)/shard_map/all_to_all | solution.py:15
  78.7 6.9 %stack.2 = bf16[32,1,1536,128]{2,3,1,0:T(8,128)(2,1)} broadcast(bf16[1536,128]{0,1:T(8,128)(2,1)} %copy.31), dimensions={2,3} | broadcast | bytes 12976128 | tf_op jit(solution)/shard_map/stack | solution.py:56
  85.6 9.1 %all-to-all-start.1 = ((bf16[32,1,1536,128]{2,3,1,0:T(8,128)(2,1)}), bf16[32,1,1536,128]{2,3,1,0:T(8,128)(2,1)}, u32[]{:S(2)}, u32[]{:S(2)}) async-start(bf16[32,1,1536,128]{2,3,1,0:T(8,128)(2,1)} %stack.2), calls=%async_computation.1 | async-start | bytes 25165824 | tf_op jit(solution)/shard_map/all_to_all | solution.py:56
  94.7 2.7 fusion.3
  97.4 0.1 convert_reduce_fusion
  97.6 1.6 split.8
  99.3 274.5 %all-to-all-done.1 = bf16[32,1,1536,128]{2,3,1,0:T(8,128)(2,1)} async-done(((bf16[32,1,1536,128]{2,3,1,0:T(8,128)(2,1)}), bf16[32,1,1536,128]{2,3,1,0:T(8,128)(2,1)}, u32[]{:S(2)}, u32[]{:S(2)}) %all-to-all-start.1) | async-done | bytes 12582944 | tf_op jit(solution)/shard_map/all_to_all | solution.py:56
  373.8 9.9 %fusion.10 = (bf16[1,1,256,1536]{3,2,1,0:T(8,128)(2,1)S(1)}, bf16[1,1,256,1536]{3,2,1,0:T(8,128)(2,1)S(1)}, f32[256]{0:T(256)S(1)}) fusion(f32[256]{0:T(256)S(1)} %reshape.73, bf16[1,1,256,3072]{3,2,1,0:T(8,128)(2,1)} %param.8, bf16[256,1536]{1,0:T(8,128)(2,1)} %fusion.3, bf16[256,4096]{1,0:T(8,128)(2,1)} %bitcast.54, bf16[1536,4096]{0,1:T(8,128)(2,1)} %bitcast.12), kind=kOutput, calls=%fused_computation.20 | convolution fusion | flops 3228696320 | bytes 18614272 | tf_op jit(solution)/shard_map/dot_general | solution.py:53
  383.7 0.7 all_to_all.16
  384.4 19.5 %all-to-all-start.2 = ((f32[16,1,16]{2,1,0:T(1,128)}), f32[16,1,16]{2,1,0:T(1,128)S(1)}, u32[]{:S(2)}, u32[]{:S(2)}) async-start(f32[16,1,16]{2,1,0:T(1,128)} %all_to_all.16), calls=%async_computation.2 | async-start | bytes 16384 | tf_op jit(solution)/shard_map/all_to_all | solution.py:72
  403.9 1.4 pad_maximum_fusion.1
  405.3 9.9 %all-to-all-done.2 = f32[16,1,16]{2,1,0:T(1,128)S(1)} async-done(((f32[16,1,16]{2,1,0:T(1,128)}), f32[16,1,16]{2,1,0:T(1,128)S(1)}, u32[]{:S(2)}, u32[]{:S(2)}) %all-to-all-start.2) | async-done | bytes 1056 | tf_op jit(solution)/shard_map/all_to_all | solution.py:72
  415.2 0.2 fusion.12
  415.4 0.6 select_reduce_fusion
  (10 shorter events, 0.3 us)
Async XLA Ops:
  0.6 3.0 copy-start
  5.9 72.8 %all-to-all-start = ((bf16[16,16,4097]{2,1,0:T(8,128)(2,1)}), bf16[16,16,4097]{2,1,0:T(8,128)(2,1)S(1)}, u32[]{:S(2)}, u32[]{:S(2)}) async-start(bf16[16,16,4097]{2,1,0:T(8,128)(2,1)} %pad_maximum_fusion), calls=%async_computation | async-start | bytes 4325376 | tf_op jit(solution)/shard_map/all_to_all | solution.py:15
  85.6 288.2 %all-to-all-start.1 = ((bf16[32,1,1536,128]{2,3,1,0:T(8,128)(2,1)}), bf16[32,1,1536,128]{2,3,1,0:T(8,128)(2,1)}, u32[]{:S(2)}, u32[]{:S(2)}) async-start(bf16[32,1,1536,128]{2,3,1,0:T(8,128)(2,1)} %stack.2), calls=%async_computation.1 | async-start | bytes 25165824 | tf_op jit(solution)/shard_map/all_to_all | solution.py:56
  384.4 30.8 %all-to-all-start.2 = ((f32[16,1,16]{2,1,0:T(1,128)}), f32[16,1,16]{2,1,0:T(1,128)S(1)}, u32[]{:S(2)}, u32[]{:S(2)}) async-start(f32[16,1,16]{2,1,0:T(1,128)} %all_to_all.16), calls=%async_computation.2 | async-start | bytes 16384 | tf_op jit(solution)/shard_map/all_to_all | solution.py:72
